TPU v7x, 256 devices: a whole 4x4x8 slice. The times are simulated.
256 devices in a mesh: row: 16 (over x_lo, y, core), col: 16 (over z, x_hi).
Axes of the slice: x: 4 (x_hi: 2, x_lo: 2; x = x_hi * 2 + x_lo), y: 4, z: 8, core: 2. Of those that a mesh axis runs over, the one named last changes fastest.
Arguments:
- green: bfloat16 [32768, 32768], P('row', 'col'), may hold values from -0.046875 to 0.046875
- mask: int32 [128, 128], P('row', 'col'), may hold values from 0 to 1, as said below
- probes: bfloat16 [32768, 256], P('col', 'row'), may hold values from -6 to 6
Outputs:
- sketch: float32 [32768, 256], P('row', 'col')
- adjoint: float32 [32768, 256], P('col', 'row')
Inputs may be any that keep to these rules, and one draw needn't show every extreme that they name: `mask`: block row i belongs to gauge i % 6 and time block i // 6; block column j to window j // 8. A block is 1 when its time block is no earlier than the window's onset plus a travel delay of its gauge and subfault block.
All inputs are finite; a program needn't handle non-finite values.
Results may differ from a plain program's by a relative error of at most 0.0022.
Values may be sent and summed in bfloat16 or wider, within the bound.
A program may use at most 128 MiB of HBM per device.

v0:
```python
import jax
import jax.numpy as jnp
from jax import lax
from jax.sharding import PartitionSpec as P


def local(green, mask, probes):
    row_blocks, col_blocks = mask.shape
    block_size = green.shape[0] // row_blocks
    shaped = green.reshape(row_blocks, block_size, col_blocks, block_size)
    tiles = (shaped * mask.astype(jnp.bfloat16)[:, None, :, None]).reshape(green.shape)
    partial_sketch = jnp.dot(
        tiles, lax.all_gather(probes, "row", axis=1, tiled=True), preferred_element_type=jnp.float32
    )
    summed = lax.psum(partial_sketch, "col")
    width_own = summed.shape[1] // lax.axis_size("col")
    own_sketch = lax.dynamic_slice_in_dim(summed, lax.axis_index("col") * width_own, width_own, 1)
    term = lax.dot_general(
        tiles,
        summed.astype(jnp.bfloat16),
        (((0,), (0,)), ((), ())),
        preferred_element_type=jnp.float32,
    )
    adjoint = lax.psum_scatter(term, "row", scatter_dimension=1, tiled=True)
    return (own_sketch, adjoint)


def solution(mesh):
    in_specs = (P("row", "col"), P("row", "col"), P("col", "row"))
    out_specs = (P("row", "col"), P("col", "row"))
    return jax.shard_map(local, mesh=mesh, in_specs=in_specs, out_specs=out_specs, check_vma=False)
```

profile of v0, /device:TPU:32, one launch (start us, length us, event | category | flops | bytes accessed | tf_op | source)
XLA Modules:
  0.0 299.5 jit_solution(3500955319090247931)
XLA Ops:
  7.2 0.0 all-gather.2.cloned.1.call-start
  7.2 0.7 all-gather.2.cloned.1.call-update
  7.9 0.0 all-reduce.2.cloned.1.call-start
  7.9 0.7 convert_element_type.6
  8.6 3.8 %mul.14 = bf16[8,256,8,256]{3,2,1,0:T(8,128)(2,1)} broadcast(bf16[8,8]{1,0:T(8,128)(2,1)S(1)} %convert_element_type.6), dimensions={0,2} | broadcast | bytes 8388736 | tf_op jit(solution)/shard_map/mul | solution.py:11
  12.5 10.3 %copy.6 = bf16[256,8,8,256]{3,1,2,0:T(8,128)(2,1)} copy(bf16[256,8,8,256]{3,2,1,0:T(8,128)(2,1)} %bitcast.7) | data formatting | bytes 16777216
  22.7 10.5 %mul.16 = bf16[2048,2048]{1,0:T(8,128)(2,1)} multiply(bf16[2048,2048]{1,0:T(8,128)(2,1)} %param.3, bf16[2048,2048]{1,0:T(8,128)(2,1)} %bitcast.6) | non-fusion elementwise | flops 4194304 | bytes 25165824 | tf_op jit(solution)/shard_map/mul | solution.py:11
  33.3 14.2 %all-gather.2.cloned.1.call-done = bf16[2048,256]{0,1:T(8,128)(2,1)} async-done(((bf16[2048,16]{0,1:T(8,128)(2,1)}), bf16[2048,256]{0,1:T(8,128)(2,1)}) %all-gather.2.cloned.1.call-update) | async-done | bytes 1048592 | tf_op jit(solution)/shard_map/all_gather | solution.py:13
  47.5 7.3 %fusion.2 = f32[2048,256]{1,0:T(8,128)} fusion(bf16[2048,2048]{1,0:T(8,128)(2,1)} %mul.16, bf16[2048,256]{0,1:T(8,128)(2,1)} %all-gather.2.cloned.1.call-done), kind=kOutput, calls=%fused_computation.3 | convolution fusion | flops 2147483648 | bytes 11534336 | tf_op jit(solution)/shard_map/dot_general | solution.py:12
  54.8 0.0 all-reduce.2.cloned.1.call-update
  54.8 0.0 reduce-scatter.2.cloned.1.call-start
  54.9 166.0 %all-reduce.2.cloned.1.call-done = f32[2048,256]{1,0:T(8,128)} async-done(((f32[2048,256]{1,0:T(8,128)}), f32[2048,256]{1,0:T(8,128)}) %all-reduce.2.cloned.1.call-update) | async-done | bytes 2097168 | tf_op jit(solution)/shard_map/psum | solution.py:15
  220.9 0.0 copy-start
  220.9 7.8 %fusion = f32[2048,256]{0,1:T(8,128)} fusion(bf16[2048,2048]{1,0:T(8,128)(2,1)} %mul.16, f32[2048,256]{1,0:T(8,128)} %all-reduce.2.cloned.1.call-done), kind=kOutput, calls=%fused_computation | convolution fusion | flops 2148007936 | bytes 12582912 | tf_op jit(solution)/shard_map/dot_general | solution.py:18
  228.7 0.0 reduce-scatter.2.cloned.1.call-update
  228.7 0.0 copy-done
  228.7 0.3 constant_dynamic-slice_fusion
  229.1 1.0 copy.5
  230.0 62.9 %reduce-scatter.2.cloned.1.call-done = f32[2048,16]{0,1:T(8,128)} async-done(((f32[2048,256]{0,1:T(8,128)}), f32[2048,16]{0,1:T(8,128)}) %reduce-scatter.2.cloned.1.call-update) | async-done | bytes 131088 | tf_op jit(solution)/shard_map/reduce_scatter | solution.py:24
Async XLA Ops:
  7.2 40.3 %all-gather.2.cloned.1.call-start = ((), (), s32[]{:S(2)}) async-start(), calls=%async_computation.1 | async-start | bytes 1114112 | tf_op jit(solution)/shard_map/all_gather | solution.py:13
  7.9 213.0 %all-reduce.2.cloned.1.call-start = ((), (), s32[]{:S(2)}) async-start(), calls=%async_computation.2 | async-start | bytes 4194304 | tf_op jit(solution)/shard_map/psum | solution.py:15
  54.8 238.2 %reduce-scatter.2.cloned.1.call-start = ((), (), s32[]{:S(2)}) async-start(), calls=%async_computation.3 | async-start | bytes 2228224 | tf_op jit(solution)/shard_map/reduce_scatter | solution.py:24
  220.9 7.8 %copy-start = (f32[2048,256]{1,0:T(8,128)S(1)}, f32[2048,256]{1,0:T(8,128)}, u32[]{:S(2)}) copy-start(f32[2048,256]{1,0:T(8,128)} %all-reduce.2.cloned.1.call-done) | copy-start | bytes 6291460
Sparse Core Ops, SparseCore 0:
  9.8 37.5 all-gather.1
  54.9 165.8 all-reduce.1
  228.8 64.0 reduce-scatter.1
where the time goes:
time: 300 us
  waiting for transfers between devices  244 us (81%)
  local copies, waits for them, and re-layouts  15.4 us (5%)
  matrix products  15.1 us (5%)
  between operations  13.8 us (5%)
  other arithmetic  11.2 us (4%)
    psum x1, waiting for transfers between devices, local(): summed = lax.psum(partial_sketch, 'col')  166 us
    reduce_scatter x1, waiting for transfers between devices, local(): adjoint = lax.psum_scatter(term, 'row', scatter_dimension=1, tiled=True)  62.9 us
    all_gather x1, waiting for transfers between devices, local(): lax.all_gather(probes, 'row', axis=1, tiled=True)  14.2 us
    unnamed x4, local copies, waits for them, and re-layouts  11.2 us
    mul x1, other arithmetic, local(): shaped * mask.astype(jnp.bfloat16)[:, None, :, None]  10.5 us
    dot_general x1, matrix products, local(): lax.dot_general(tiles, summed.astype(jnp.bfloat16), (((0,), (0,)), ((), (...  7.8 us
    dot_general x1, matrix products, local(): jnp.dot(tiles, lax.all_gather(probes, 'row', axis=1, tiled=True), preferr...  7.31 us
  transfers between devices with their start and end apart: 3, of which 3 were waited for; matrix products, arithmetic and copies ran while one was open for 9% of the time, Pallas kernels for 0%

commit v1 on v0

--- a/solution.py
+++ b/solution.py
@@ -12,7 +12,8 @@
     partial_sketch = jnp.dot(
         tiles, lax.all_gather(probes, "row", axis=1, tiled=True), preferred_element_type=jnp.float32
     )
-    summed = lax.psum(partial_sketch, "col")
+    small = jax.lax.all_gather(partial_sketch, axis_name="col")
+    summed = jnp.sum(small, 0)
     width_own = summed.shape[1] // lax.axis_size("col")
     own_sketch = lax.dynamic_slice_in_dim(summed, lax.axis_index("col") * width_own, width_own, 1)
     term = lax.dot_general(

time: 300 us -> 557 us (1.86)
  waiting for transfers between devices: 244 us -> 490 us
  other arithmetic: 11.2 us -> 23.3 us
    all_gather x0 -> x1, waiting for transfers between devices: none -> 412 us  [local(): small = jax.lax.all_gather(partial_sketch, axis_name='col')]
    psum x1 -> x0, waiting for transfers between devices: 166 us -> none  [local(): summed = lax.psum(partial_sketch, 'col')]
    reduce_sum x0 -> x1, other arithmetic: none -> 12.1 us  [local(): summed = jnp.sum(small, 0)]
    unnamed x4 -> x2, local copies, waits for them, and re-layouts: 11.2 us -> 11.2 us
  transfers between devices with their start and end apart: 3 -> 3, of which waited for: 3 -> 3; matrix products, arithmetic and copies ran while one was open for 9% -> 5% of each run, Pallas kernels for 0% -> 0%
where the time goes in v1:
time: 557 us
  waiting for transfers between devices  490 us (88%)
  other arithmetic  23.3 us (4%)
  local copies, waits for them, and re-layouts  15.4 us (3%)
  matrix products  14.4 us (3%)
  between operations  13.8 us (2%)
    all_gather x1, waiting for transfers between devices, local(): small = jax.lax.all_gather(partial_sketch, axis_name='col')  412 us
    reduce_scatter x1, waiting for transfers between devices, local(): adjoint = lax.psum_scatter(term, 'row', scatter_dimension=1, tiled=True)  63.3 us
    all_gather x1, waiting for transfers between devices, local(): lax.all_gather(probes, 'row', axis=1, tiled=True)  14.2 us
    reduce_sum x1, other arithmetic, local(): summed = jnp.sum(small, 0)  12.1 us
    unnamed x2, local copies, waits for them, and re-layouts  11.2 us
  transfers between devices with their start and end apart: 3, of which 3 were waited for; matrix products, arithmetic and copies ran while one was open for 5% of the time, Pallas kernels for 0%

profile of v1, /device:TPU:32, one launch (start us, length us, event | category | flops | bytes accessed | tf_op | source)
XLA Modules:
  0.0 556.8 jit_solution(11488618515080273063)
XLA Ops:
  7.2 0.0 all-gather.4.cloned.1.call-start
  7.2 0.7 all-gather.4.cloned.1.call-update
  7.9 0.0 all-gather.6.cloned.1.call-start
  7.9 0.7 convert_element_type.6
  8.6 3.8 mul.14
  12.5 10.3 %copy.6 = bf16[256,8,8,256]{3,1,2,0:T(8,128)(2,1)} copy(bf16[256,8,8,256]{3,2,1,0:T(8,128)(2,1)} %bitcast.9) | data formatting | bytes 16777216
  22.7 10.5 %mul.16 = bf16[2048,2048]{1,0:T(8,128)(2,1)} multiply(bf16[2048,2048]{1,0:T(8,128)(2,1)} %param.3, bf16[2048,2048]{1,0:T(8,128)(2,1)} %bitcast.7) | non-fusion elementwise | flops 4194304 | bytes 25165824 | tf_op jit(solution)/shard_map/mul | solution.py:11
  33.2 14.2 %all-gather.4.cloned.1.call-done = bf16[2048,256]{0,1:T(8,128)(2,1)} async-done(((bf16[2048,16]{0,1:T(8,128)(2,1)}), bf16[2048,256]{0,1:T(8,128)(2,1)}) %all-gather.4.cloned.1.call-update) | async-done | bytes 1048592 | tf_op jit(solution)/shard_map/all_gather | solution.py:13
  47.5 7.4 %fusion.2 = f32[2048,256]{1,0:T(8,128)} fusion(bf16[2048,2048]{1,0:T(8,128)(2,1)} %mul.16, bf16[2048,256]{0,1:T(8,128)(2,1)} %all-gather.4.cloned.1.call-done), kind=kOutput, calls=%fused_computation.3 | convolution fusion | flops 2147483648 | bytes 11534336 | tf_op jit(solution)/shard_map/dot_general | solution.py:12
  54.8 0.0 all-gather.6.cloned.1.call-update
  54.9 0.0 reduce-scatter.2.cloned.1.call-start
  54.9 411.5 %all-gather.6.cloned.1.call-done = f32[32768,256]{1,0:T(8,128)} async-done(((f32[2048,256]{1,0:T(8,128)}), f32[32768,256]{1,0:T(8,128)}) %all-gather.6.cloned.1.call-update) | async-done | bytes 33554448 | tf_op jit(solution)/shard_map/all_gather | solution.py:15
  466.4 12.1 %reduce_sum.9 = f32[2048,256]{1,0:T(8,128)S(1)} reduce(f32[16,2048,256]{2,1,0:T(8,128)} %bitcast.8, f32[]{:T(128)} %constant.5.clone.1), dimensions={0}, to_apply=%region_0.0 | reduce | flops 7864320 | bytes 35651588 | tf_op jit(solution)/shard_map/reduce_sum | solution.py:16
  478.5 7.1 %fusion = f32[2048,256]{0,1:T(8,128)} fusion(bf16[2048,2048]{1,0:T(8,128)(2,1)} %mul.16, f32[2048,256]{1,0:T(8,128)S(1)} %reduce_sum.9), kind=kOutput, calls=%fused_computation | convolution fusion | flops 2148007936 | bytes 12582912 | tf_op jit(solution)/shard_map/dot_general | solution.py:19
  485.6 0.0 reduce-scatter.2.cloned.1.call-update
  485.6 0.3 constant_dynamic-slice_fusion
  486.0 1.0 copy.5
  486.9 63.3 %reduce-scatter.2.cloned.1.call-done = f32[2048,16]{0,1:T(8,128)} async-done(((f32[2048,256]{0,1:T(8,128)}), f32[2048,16]{0,1:T(8,128)}) %reduce-scatter.2.cloned.1.call-update) | async-done | bytes 131088 | tf_op jit(solution)/shard_map/reduce_scatter | solution.py:25
Async XLA Ops:
  7.2 40.3 %all-gather.4.cloned.1.call-start = ((), (), s32[]{:S(2)}) async-start(), calls=%async_computation.1 | async-start | bytes 1114112 | tf_op jit(solution)/shard_map/all_gather | solution.py:13
  7.9 458.5 %all-gather.6.cloned.1.call-start = ((), (), s32[]{:S(2)}) async-start(), calls=%async_computation.3 | async-start | bytes 35651584 | tf_op jit(solution)/shard_map/all_gather | solution.py:15
  54.9 495.4 %reduce-scatter.2.cloned.1.call-start = ((), (), s32[]{:S(2)}) async-start(), calls=%async_computation.2 | async-start | bytes 2228224 | tf_op jit(solution)/shard_map/reduce_scatter | solution.py:25
Sparse Core Ops, SparseCore 0:
  9.8 37.5 all-gather.3
  55.0 411.3 all-gather.5
  485.7 64.4 reduce-scatter.1
